TPU v7x, 512 devices: a whole 4x8x8 slice. The times are simulated.
512 devices in a mesh: dp: 64 (over y, z_lo, core), tensor: 8 (over z_hi, x).
Axes of the slice: x: 4, y: 8, z: 8 (z_hi: 2, z_lo: 4; z = z_hi * 4 + z_lo), core: 2. Of those that a mesh axis runs over, the one named last changes fastest.
Arguments:
- layer_input: bfloat16 [2, 4096, 8192], P(None, ('dp', 'tensor')), may hold values from -6 to 6
- key_gradient_rows: bfloat16 [2, 4096, 1024], P(None, 'dp', 'tensor'), may hold values from -6 to 6
- key_block_matrix: bfloat16 [8, 6144, 128], P('tensor', 'dp'), may hold values from -0.09375 to 0.09375
- kept_rows: int32 [8, 48], replicated, may hold values from -1 to 63, as said below
Outputs:
- weight_grad: float32 [8, 6144, 128], P('tensor', 'dp')
- input_grad: bfloat16 [2, 4096, 8192], P(None, ('dp', 'tensor'))
Inputs may be any that keep to these rules, and one draw needn't show every extreme that they name: `kept_rows`: row h lists in ascending order the distinct blocks (of the 64 blocks of 128 input rows) that survive pruning for head h, then -1 in its unused slots. At most 48 blocks survive for one head and exactly 48 for some head; 256 blocks survive in all, at least one for every head.
All inputs are finite; a program needn't handle non-finite values.
Results may differ from a plain program's by a relative error of at most 0.005.
Values may be sent and summed in bfloat16 or wider, within the bound.
A program may use at most 64 MiB of HBM per device.

v0:
```python
import math
import jax
import jax.numpy as jnp
from jax import lax
from jax.sharding import PartitionSpec as P

MODEL_WIDTH = 8192
HEAD_WIDTH = 128
PRUNE_BLOCK_ROWS = 128
HEAD_BLOCK_LIMIT = 48
MICRO_BATCHES = 2


def local(layer_input, key_gradient_rows, key_block_matrix, kept_rows):
    my_head = lax.axis_index("tensor")
    groups = lax.axis_size("tensor")
    block_count = MODEL_WIDTH // PRUNE_BLOCK_ROWS
    own_rows = lax.dynamic_index_in_dim(kept_rows, my_head, 0, keepdims=False)
    alive = own_rows >= 0
    clipped = jnp.maximum(own_rows, 0)
    gathered_w = lax.all_gather(key_block_matrix, "dp", axis=1, tiled=True)
    blocks_w = gathered_w.reshape(HEAD_BLOCK_LIMIT, PRUNE_BLOCK_ROWS, HEAD_WIDTH) * alive[
        :, None, None
    ].astype(jnp.bfloat16)
    placing = (kept_rows[:, :, None] == jnp.arange(block_count)[None, None, :]).astype(jnp.bfloat16)
    accum = jnp.zeros((HEAD_BLOCK_LIMIT, PRUNE_BLOCK_ROWS, HEAD_WIDTH), jnp.float32)
    results = []
    for micro in range(MICRO_BATCHES):
        grads_here = key_gradient_rows[micro]
        group_x = lax.all_gather(layer_input[micro], "tensor", axis=0, tiled=True)
        picked = jnp.take(
            group_x.reshape(group_x.shape[0], block_count, PRUNE_BLOCK_ROWS), clipped, axis=1
        )
        product = jnp.einsum("gcb,gh->cbh", picked, grads_here, preferred_element_type=jnp.float32)
        accum = accum + product * alive[:, None, None].astype(jnp.float32)
        partial_value = jnp.einsum(
            "gh,cbh->gcb", grads_here, blocks_w, preferred_element_type=jnp.float32
        ).astype(jnp.bfloat16)
        partial_value = partial_value.reshape(
            grads_here.shape[0], 1, HEAD_BLOCK_LIMIT * PRUNE_BLOCK_ROWS
        )
        received = lax.all_to_all(partial_value, "tensor", split_axis=0, concat_axis=1, tiled=True)
        own_tokens = received.shape[0]
        received = received.reshape(own_tokens, groups, HEAD_BLOCK_LIMIT, PRUNE_BLOCK_ROWS)
        summed = jnp.einsum("tkcb,kcn->tnb", received, placing, preferred_element_type=jnp.float32)
        results.append(summed.reshape(own_tokens, MODEL_WIDTH).astype(jnp.bfloat16))
    owned = lax.psum_scatter(
        accum.reshape(HEAD_BLOCK_LIMIT * PRUNE_BLOCK_ROWS, HEAD_WIDTH),
        "dp",
        scatter_dimension=0,
        tiled=True,
    )
    scale = 1.0 / math.sqrt(MICRO_BATCHES * key_gradient_rows.shape[1] * lax.axis_size("dp"))
    weight_grad = (owned * scale)[None, :, :]
    return (weight_grad, jnp.stack(results))


def solution(mesh):
    placed = (
        P(None, ("dp", "tensor"), None),
        P(None, "dp", "tensor"),
        P("tensor", "dp", None),
        P(),
    )
    return jax.shard_map(
        local,
        mesh=mesh,
        in_specs=placed,
        out_specs=(P("tensor", "dp", None), P(None, ("dp", "tensor"), None)),
        check_vma=False,
    )
```

profile of v0, /device:TPU:6, one launch (start us, length us, event | category | flops | bytes accessed | tf_op | source)
XLA Modules:
  0.0 561.7 jit_solution(8836301085394832991)
XLA Ops:
  7.2 0.0 all-gather.10.cloned.1.call-start
  7.2 1.7 fusion.36
  8.9 0.0 all-gather.10.cloned.1.call-update
  8.9 0.0 all-gather.8.cloned.1.call-start
  9.0 0.7 all-gather.8.cloned.1.call-update
  9.7 0.0 all-gather.6.cloned.1.call-start
  9.7 0.7 all-gather.6.cloned.1.call-update
  10.4 0.0 reduce-scatter.2.cloned.1.call-start
  10.4 0.7 fusion.32
  11.1 0.7 compare_and_fusion
  11.8 72.0 %all-gather.10.cloned.1.call-done = bf16[1,64,8192]{2,1,0:T(8,128)(2,1)} async-done(((bf16[1,8,8192]{2,1,0:T(8,128)(2,1)}), bf16[1,64,8192]{2,1,0:T(8,128)(2,1)}) %all-gather.10.cloned.1.call-update) | async-done | bytes 1048592 | tf_op jit(solution)/shard_map/all_gather | solution.py:30
  83.8 1.5 copy.31
  85.3 0.7 copy.17
  86.0 64.4 %all-gather.8.cloned.1.call-done = bf16[1,64,8192]{2,1,0:T(8,128)(2,1)} async-done(((bf16[1,8,8192]{2,1,0:T(8,128)(2,1)}), bf16[1,64,8192]{2,1,0:T(8,128)(2,1)}) %all-gather.8.cloned.1.call-update) | async-done | bytes 1048592 | tf_op jit(solution)/shard_map/all_gather | solution.py:30
  150.5 1.5 copy.30
  152.0 0.7 copy.16
  152.7 0.0 copy-start
  152.7 0.7 gather_fusion.1
  153.4 0.7 gather_fusion
  154.1 0.0 copy-done
  154.1 0.8 fusion.11
  154.9 2.8 add_multiply_fusion
  157.7 0.0 reduce-scatter.2.cloned.1.call-update
  157.7 0.1 broadcast_bitcast_fusion
  157.8 109.0 %all-gather.6.cloned.1.call-done = bf16[1,6144,128]{2,1,0:T(8,128)(2,1)} async-done(((bf16[1,96,128]{2,1,0:T(8,128)(2,1)}), bf16[1,6144,128]{2,1,0:T(8,128)(2,1)}) %all-gather.6.cloned.1.call-update) | async-done | bytes 1572880 | tf_op jit(solution)/shard_map/all_gather | solution.py:21
  266.8 2.1 broadcast_multiply_fusion
  268.9 0.7 fusion.1
  269.6 1.4 copy.21
  271.0 4.4 reshape.124
  275.4 0.5 broadcast.58
  275.9 6.2 %reduce = bf16[64,6144]{1,0:T(8,128)(2,1)} reduce(bf16[64,1,6144]{2,1,0:T(2,128)(2,1)S(1)} %reshape.124, bf16[]{:T(256)} %broadcast.58), dimensions={1}, to_apply=%reshape.124.reduce_sub_computation | reduce | bytes 1572866 | tf_op jit(solution)/shard_map/reshape | solution.py:39
  282.2 3.2 reshape.126
  285.3 8.2 %all-to-all-start.1 = ((bf16[8,2,24576]{2,1,0:T(2,128)(2,1)}), bf16[8,2,24576]{2,1,0:T(2,128)(2,1)S(1)}, u32[]{:S(2)}, u32[]{:S(2)}) async-start(bf16[8,2,24576]{2,1,0:T(2,128)(2,1)} %reshape.126), calls=%async_computation.2 | async-start | bytes 1572864 | tf_op jit(solution)/shard_map/all_to_all | solution.py:42
  293.6 0.7 fusion
  294.2 1.4 copy.18
  295.6 4.4 reshape.122
  300.1 5.4 reduce.1
  305.4 1.7 reshape.128
  307.1 5.2 all-to-all-done.1
  312.3 4.9 all-to-all-start
  317.2 0.8 reshape.127
  318.0 0.0 copy-start.1
  318.0 0.4 copy.44
  318.5 0.2 copy-done.1
  318.7 0.4 fusion.4
  319.2 0.1 convert_element_type.78
  319.2 13.0 %all-to-all-done = bf16[8,2,24576]{2,1,0:T(2,128)(2,1)S(1)} async-done(((bf16[8,2,24576]{2,1,0:T(2,128)(2,1)}), bf16[8,2,24576]{2,1,0:T(2,128)(2,1)S(1)}, u32[]{:S(2)}, u32[]{:S(2)}) %all-to-all-start) | async-done | bytes 786464 | tf_op jit(solution)/shard_map/all_to_all | solution.py:42
  332.2 0.8 reshape.129
  333.0 0.4 copy.45
  333.5 0.4 fusion.5
  333.9 0.1 convert_element_type.73
  334.0 0.7 pad_maximum_fusion
  334.7 219.0 %reduce-scatter.2.cloned.1.call-done = f32[96,128]{1,0:T(8,128)} async-done(((f32[6144,128]{1,0:T(8,128)}), f32[96,128]{1,0:T(8,128)}) %reduce-scatter.2.cloned.1.call-update) | async-done | bytes 49168 | tf_op jit(solution)/shard_map/reduce_scatter | solution.py:47
  553.7 1.4 multiply_bitcast_fusion
  (1 shorter events, 0.0 us)
Async XLA Ops:
  7.2 76.7 %all-gather.10.cloned.1.call-start = ((), (), s32[]{:S(2)}) async-start(), calls=%async_computation.6 | async-start | bytes 1179648 | tf_op jit(solution)/shard_map/all_gather | solution.py:30
  8.9 141.6 %all-gather.8.cloned.1.call-start = ((), (), s32[]{:S(2)}) async-start(), calls=%async_computation.5 | async-start | bytes 1179648 | tf_op jit(solution)/shard_map/all_gather | solution.py:30
  9.7 257.1 %all-gather.6.cloned.1.call-start = ((), (), s32[]{:S(2)}) async-start(), calls=%async_computation.4 | async-start | bytes 1597440 | tf_op jit(solution)/shard_map/all_gather | solution.py:21
  10.4 543.3 %reduce-scatter.2.cloned.1.call-start = ((), (), s32[]{:S(2)}) async-start(), calls=%async_computation.3 | async-start | bytes 3194880 | tf_op jit(solution)/shard_map/reduce_scatter | solution.py:47
  152.7 1.4 copy-start
  285.3 27.0 %all-to-all-start.1 = ((bf16[8,2,24576]{2,1,0:T(2,128)(2,1)}), bf16[8,2,24576]{2,1,0:T(2,128)(2,1)S(1)}, u32[]{:S(2)}, u32[]{:S(2)}) async-start(bf16[8,2,24576]{2,1,0:T(2,128)(2,1)} %reshape.126), calls=%async_computation.2 | async-start | bytes 1572864 | tf_op jit(solution)/shard_map/all_to_all | solution.py:42
  312.3 19.9 %all-to-all-start = ((bf16[8,2,24576]{2,1,0:T(2,128)(2,1)}), bf16[8,2,24576]{2,1,0:T(2,128)(2,1)S(1)}, u32[]{:S(2)}, u32[]{:S(2)}) async-start(bf16[8,2,24576]{2,1,0:T(2,128)(2,1)} %reshape.128), calls=%async_computation.1 | async-start | bytes 1572864 | tf_op jit(solution)/shard_map/all_to_all | solution.py:42
  318.0 0.7 copy-start.1
Sparse Core Ops, SparseCore 0:
  11.8 72.0 all-gather.9
  87.0 63.3 all-gather.7
  152.6 114.1 all-gather.5
  269.4 284.2 reduce-scatter.1
where the time goes:
time: 562 us
  waiting for transfers between devices  484 us (86%)
  local copies, waits for them, and re-layouts  27.4 us (5%)
  other arithmetic  17.2 us (3%)
  between operations  14 us (2%)
  starting transfers between devices  13.3 us (2%)
  matrix products  5.81 us (1%)
    reduce_scatter x1, waiting for transfers between devices, local(): lax.psum_scatter(accum.reshape(HEAD_BLOCK_LIMIT * PRUNE_BLOCK_ROWS, HEAD_...  219 us
    all_gather x2, waiting for transfers between devices, local(): group_x = lax.all_gather(layer_input[micro], 'tensor', axis=0, tiled=True)  136 us
    all_gather x1, waiting for transfers between devices, local(): gathered_w = lax.all_gather(key_block_matrix, 'dp', axis=1, tiled=True)  109 us
    all_to_all x2, waiting for transfers between devices, local(): lax.all_to_all(partial_value, 'tensor', split_axis=0, concat_axis=1, tile...  18.1 us
    all_to_all x2, starting transfers between devices, local(): lax.all_to_all(partial_value, 'tensor', split_axis=0, concat_axis=1, tile...  13.1 us
    reshape x2, other arithmetic, local(): partial_value.reshape(grads_here.shape[0], 1, HEAD_BLOCK_LIMIT * PRUNE_BL...  11.6 us
  transfers between devices with their start and end apart: 6, of which 6 were waited for; matrix products, arithmetic and copies ran while one was open for 8% of the time, Pallas kernels for 0%

commit v1 on v0

--- a/solution.py
+++ b/solution.py
@@ -27,7 +27,12 @@
     results = []
     for micro in range(MICRO_BATCHES):
         grads_here = key_gradient_rows[micro]
-        group_x = lax.all_gather(layer_input[micro], "tensor", axis=0, tiled=True)
+        group_x = jnp.concatenate(
+            lax.all_to_all(
+                jnp.stack([layer_input[micro]] * lax.axis_size("tensor")), "tensor", 0, 0
+            ),
+            axis=0,
+        )
         picked = jnp.take(
             group_x.reshape(group_x.shape[0], block_count, PRUNE_BLOCK_ROWS), clipped, axis=1
         )

time: 562 us -> 462 us (0.82)
  waiting for transfers between devices: 484 us -> 353 us
  starting transfers between devices: 13.3 us -> 46.4 us
    all_gather x2 -> x0, waiting for transfers between devices: 136 us -> none  [local(): group_x = lax.all_gather(layer_input[micro], 'tensor', axis=0, tiled=True)]
    all_to_all x0 -> x2, waiting for transfers between devices: none -> 29.1 us  [local(): lax.all_to_all(jnp.stack([layer_input[micro]] * lax.axis_size('tensor')),...]
    all_to_all x0 -> x2, starting transfers between devices: none -> 28.5 us  [local(): lax.all_to_all(jnp.stack([layer_input[micro]] * lax.axis_size('tensor')),...]
    all_gather x1, waiting for transfers between devices: 109 us -> 84.5 us  [local(): gathered_w = lax.all_gather(key_block_matrix, 'dp', axis=1, tiled=True)]
    all_to_all x2, waiting for transfers between devices: 18.1 us -> 32.8 us  [local(): lax.all_to_all(partial_value, 'tensor', split_axis=0, concat_axis=1, tile...]
    reduce_scatter x1, waiting for transfers between devices: 219 us -> 206 us  [local(): lax.psum_scatter(accum.reshape(HEAD_BLOCK_LIMIT * PRUNE_BLOCK_ROWS, HEAD_...]
  transfers between devices with their start and end apart: 6 -> 6, of which waited for: 6 -> 6; matrix products, arithmetic and copies ran while one was open for 8% -> 10% of each run, Pallas kernels for 0% -> 0%
where the time goes in v1:
time: 462 us; the launch traced here: 461 us
  waiting for transfers between devices  353 us (76%)
  starting transfers between devices  46.4 us (10%)
  local copies, waits for them, and re-layouts  26.1 us (6%)
  other arithmetic  15.9 us (3%)
  between operations  14.2 us (3%)
  matrix products  5.83 us (1%)
    reduce_scatter x1, waiting for transfers between devices, local(): lax.psum_scatter(accum.reshape(HEAD_BLOCK_LIMIT * PRUNE_BLOCK_ROWS, HEAD_...  206 us
    all_gather x1, waiting for transfers between devices, local(): gathered_w = lax.all_gather(key_block_matrix, 'dp', axis=1, tiled=True)  84.5 us
    all_to_all x2, waiting for transfers between devices, local(): lax.all_to_all(partial_value, 'tensor', split_axis=0, concat_axis=1, tile...  32.8 us
    all_to_all x2, waiting for transfers between devices, local(): lax.all_to_all(jnp.stack([layer_input[micro]] * lax.axis_size('tensor')),...  29.1 us
    all_to_all x2, starting transfers between devices, local(): lax.all_to_all(jnp.stack([layer_input[micro]] * lax.axis_size('tensor')),...  28.5 us
    all_to_all x2, starting transfers between devices, local(): lax.all_to_all(partial_value, 'tensor', split_axis=0, concat_axis=1, tile...  17.9 us
    reshape x2, other arithmetic, local(): partial_value.reshape(grads_here.shape[0], 1, HEAD_BLOCK_LIMIT * PRUNE_BL...  11.6 us
    reshape x3, local copies, waits for them, and re-layouts, local(): partial_value.reshape(grads_here.shape[0], 1, HEAD_BLOCK_LIMIT * PRUNE_BL...  9.4 us
  transfers between devices with their start and end apart: 6, of which 6 were waited for; matrix products, arithmetic and copies ran while one was open for 10% of the time, Pallas kernels for 0%

profile of v1, /device:TPU:6, one launch (start us, length us, event | category | flops | bytes accessed | tf_op | source)
XLA Modules:
  0.0 461.4 jit_solution(7894493445154762259)
XLA Ops:
  7.2 1.0 slice_bitcast_fusion
  8.2 1.0 stack.12
  9.2 13.2 %all-to-all-start.1 = ((bf16[8,8,8192]{2,1,0:T(8,128)(2,1)}), bf16[8,8,8192]{2,1,0:T(8,128)(2,1)S(1)}, u32[]{:S(2)}, u32[]{:S(2)}) async-start(bf16[8,8,8192]{2,1,0:T(8,128)(2,1)} %stack.12), calls=%async_computation.1 | async-start | bytes 2097152 | tf_op jit(solution)/shard_map/all_to_all | solution.py:31
  22.4 0.0 all-gather.2.cloned.1.call-start
  22.4 0.7 all-gather.2.cloned.1.call-update
  23.1 16.4 %all-to-all-done.1 = bf16[8,8,8192]{2,1,0:T(8,128)(2,1)S(1)} async-done(((bf16[8,8,8192]{2,1,0:T(8,128)(2,1)}), bf16[8,8,8192]{2,1,0:T(8,128)(2,1)S(1)}, u32[]{:S(2)}, u32[]{:S(2)}) %all-to-all-start.1) | async-done | bytes 1048608 | tf_op jit(solution)/shard_map/all_to_all | solution.py:31
  39.5 0.0 copy-start.1
  39.5 1.0 stack.11
  40.6 15.3 %all-to-all-start = ((bf16[8,8,8192]{2,1,0:T(8,128)(2,1)}), bf16[8,8,8192]{2,1,0:T(8,128)(2,1)S(1)}, u32[]{:S(2)}, u32[]{:S(2)}) async-start(bf16[8,8,8192]{2,1,0:T(8,128)(2,1)} %stack.11), calls=%async_computation | async-start | bytes 2097152 | tf_op jit(solution)/shard_map/all_to_all | solution.py:31
  55.9 0.0 reduce-scatter.2.cloned.1.call-start
  55.9 0.0 copy-done.1
  55.9 0.3 copy.31
  56.2 0.7 copy.17
  56.9 12.7 %all-to-all-done = bf16[8,8,8192]{2,1,0:T(8,128)(2,1)S(1)} async-done(((bf16[8,8,8192]{2,1,0:T(8,128)(2,1)}), bf16[8,8,8192]{2,1,0:T(8,128)(2,1)S(1)}, u32[]{:S(2)}, u32[]{:S(2)}) %all-to-all-start) | async-done | bytes 1048608 | tf_op jit(solution)/shard_map/all_to_all | solution.py:31
  69.6 0.3 copy.30
  69.8 0.7 copy.16
  70.5 0.0 copy-start
  70.5 0.7 gather_fusion.1
  71.3 0.7 gather_fusion
  72.0 0.0 copy-done
  72.0 0.8 fusion.11
  72.8 2.8 add_multiply_fusion
  75.6 0.0 reduce-scatter.2.cloned.1.call-update
  75.6 0.1 broadcast_bitcast_fusion
  75.7 84.5 %all-gather.2.cloned.1.call-done = bf16[1,6144,128]{2,1,0:T(8,128)(2,1)} async-done(((bf16[1,96,128]{2,1,0:T(8,128)(2,1)}), bf16[1,6144,128]{2,1,0:T(8,128)(2,1)}) %all-gather.2.cloned.1.call-update) | async-done | bytes 1572880 | tf_op jit(solution)/shard_map/all_gather | solution.py:21
  160.2 2.1 broadcast_multiply_fusion
  162.3 0.7 fusion.1
  163.0 1.4 copy.21
  164.4 4.4 reshape.114
  168.8 0.5 broadcast.60
  169.4 6.2 %reduce = bf16[64,6144]{1,0:T(8,128)(2,1)} reduce(bf16[64,1,6144]{2,1,0:T(2,128)(2,1)S(1)} %reshape.114, bf16[]{:T(256)} %broadcast.60), dimensions={1}, to_apply=%reshape.114.reduce_sub_computation | reduce | bytes 1572866 | tf_op jit(solution)/shard_map/reshape | solution.py:44
  175.6 3.2 reshape.116
  178.8 13.1 %all-to-all-start.3 = ((bf16[8,2,24576]{2,1,0:T(2,128)(2,1)}), bf16[8,2,24576]{2,1,0:T(2,128)(2,1)S(1)}, u32[]{:S(2)}, u32[]{:S(2)}) async-start(bf16[8,2,24576]{2,1,0:T(2,128)(2,1)} %reshape.116), calls=%async_computation.4 | async-start | bytes 1572864 | tf_op jit(solution)/shard_map/all_to_all | solution.py:47
  191.8 0.7 fusion
  192.5 1.4 copy.18
  193.9 4.4 reshape.112
  198.4 5.4 %reduce.1 = bf16[64,6144]{1,0:T(8,128)(2,1)S(1)} reduce(bf16[64,1,6144]{2,1,0:T(2,128)(2,1)S(1)} %reshape.112, bf16[]{:T(256)} %broadcast.60), dimensions={1}, to_apply=%reshape.112.reduce_sub_computation | reduce | bytes 1572866 | tf_op jit(solution)/shard_map/reshape | solution.py:44
  203.7 1.7 reshape.118
  205.4 10.2 %all-to-all-done.3 = bf16[8,2,24576]{2,1,0:T(2,128)(2,1)S(1)} async-done(((bf16[8,2,24576]{2,1,0:T(2,128)(2,1)}), bf16[8,2,24576]{2,1,0:T(2,128)(2,1)S(1)}, u32[]{:S(2)}, u32[]{:S(2)}) %all-to-all-start.3) | async-done | bytes 786464 | tf_op jit(solution)/shard_map/all_to_all | solution.py:47
  215.6 4.8 %all-to-all-start.2 = ((bf16[8,2,24576]{2,1,0:T(2,128)(2,1)}), bf16[8,2,24576]{2,1,0:T(2,128)(2,1)S(1)}, u32[]{:S(2)}, u32[]{:S(2)}) async-start(bf16[8,2,24576]{2,1,0:T(2,128)(2,1)} %reshape.118), calls=%async_computation.3 | async-start | bytes 1572864 | tf_op jit(solution)/shard_map/all_to_all | solution.py:47
  220.4 0.8 reshape.117
  221.2 0.4 copy.44
  221.7 0.4 fusion.4
  222.1 0.1 convert_element_type.78
  222.2 22.6 %all-to-all-done.2 = bf16[8,2,24576]{2,1,0:T(2,128)(2,1)S(1)} async-done(((bf16[8,2,24576]{2,1,0:T(2,128)(2,1)}), bf16[8,2,24576]{2,1,0:T(2,128)(2,1)S(1)}, u32[]{:S(2)}, u32[]{:S(2)}) %all-to-all-start.2) | async-done | bytes 786464 | tf_op jit(solution)/shard_map/all_to_all | solution.py:47
  244.8 0.8 reshape.119
  245.6 0.4 copy.45
  246.1 0.4 fusion.5
  246.5 0.1 convert_element_type.73
  246.6 0.7 pad_maximum_fusion
  247.3 205.8 %reduce-scatter.2.cloned.1.call-done = f32[96,128]{1,0:T(8,128)} async-done(((f32[6144,128]{1,0:T(8,128)}), f32[96,128]{1,0:T(8,128)}) %reduce-scatter.2.cloned.1.call-update) | async-done | bytes 49168 | tf_op jit(solution)/shard_map/reduce_scatter | solution.py:52
  453.1 1.4 multiply_bitcast_fusion
  (3 shorter events, 0.0 us)
Async XLA Ops:
  9.2 30.3 %all-to-all-start.1 = ((bf16[8,8,8192]{2,1,0:T(8,128)(2,1)}), bf16[8,8,8192]{2,1,0:T(8,128)(2,1)S(1)}, u32[]{:S(2)}, u32[]{:S(2)}) async-start(bf16[8,8,8192]{2,1,0:T(8,128)(2,1)} %stack.12), calls=%async_computation.1 | async-start | bytes 2097152 | tf_op jit(solution)/shard_map/all_to_all | solution.py:31
  22.4 137.8 %all-gather.2.cloned.1.call-start = ((), (), s32[]{:S(2)}) async-start(), calls=%async_computation.6 | async-start | bytes 1597440 | tf_op jit(solution)/shard_map/all_gather | solution.py:21
  39.5 16.3 %copy-start.1 = (s32[8,48]{1,0:T(8,128)S(1)}, s32[8,48]{1,0:T(8,128)}, u32[]{:S(2)}) copy-start(s32[8,48]{1,0:T(8,128)} %param.9) | copy-start | bytes 4612
  40.6 29.0 %all-to-all-start = ((bf16[8,8,8192]{2,1,0:T(8,128)(2,1)}), bf16[8,8,8192]{2,1,0:T(8,128)(2,1)S(1)}, u32[]{:S(2)}, u32[]{:S(2)}) async-start(bf16[8,8,8192]{2,1,0:T(8,128)(2,1)} %stack.11), calls=%async_computation | async-start | bytes 2097152 | tf_op jit(solution)/shard_map/all_to_all | solution.py:31
  55.9 397.2 %reduce-scatter.2.cloned.1.call-start = ((), (), s32[]{:S(2)}) async-start(), calls=%async_computation.5 | async-start | bytes 3194880 | tf_op jit(solution)/shard_map/reduce_scatter | solution.py:52
  70.5 1.4 copy-start
  178.8 36.9 %all-to-all-start.3 = ((bf16[8,2,24576]{2,1,0:T(2,128)(2,1)}), bf16[8,2,24576]{2,1,0:T(2,128)(2,1)S(1)}, u32[]{:S(2)}, u32[]{:S(2)}) async-start(bf16[8,2,24576]{2,1,0:T(2,128)(2,1)} %reshape.116), calls=%async_computation.4 | async-start | bytes 1572864 | tf_op jit(solution)/shard_map/all_to_all | solution.py:47
  215.6 29.2 %all-to-all-start.2 = ((bf16[8,2,24576]{2,1,0:T(2,128)(2,1)}), bf16[8,2,24576]{2,1,0:T(2,128)(2,1)S(1)}, u32[]{:S(2)}, u32[]{:S(2)}) async-start(bf16[8,2,24576]{2,1,0:T(2,128)(2,1)} %reshape.118), calls=%async_computation.3 | async-start | bytes 1572864 | tf_op jit(solution)/shard_map/all_to_all | solution.py:47
Sparse Core Ops, SparseCore 0:
  25.4 134.7 all-gather.1
  163.0 290.0 reduce-scatter.1
